TPU v7x, 32 devices: a whole 2x2x4 slice. The times are simulated.
32 devices in a mesh: clip: 2 (over y), tm: 4 (over z), band: 2 (over x), head: 2 (over core).
Axes of the slice: x: 2, y: 2, z: 4, core: 2. Of those that a mesh axis runs over, the one named last changes fastest.
Arguments:
- queries: bfloat16 [8, 2, 256, 1536], P(('clip', 'tm'), 'band', None, 'head'), parts along dimension 0, may hold values from -6 to 6
- keys: bfloat16 [8, 2, 256, 1536], P(('clip', 'tm'), 'band', None, 'head'), parts along dimension 0, may hold values from -6 to 6
- values: bfloat16 [8, 2, 256, 1536], P(('clip', 'tm'), 'band', None, 'head'), parts along dimension 0, may hold values from -6 to 6
- adj_mask: int32 [8, 2, 2, 2], P(('clip', 'tm'), 'band'), parts along dimension 0, may hold values from 0 to 1, as said below
- border_blocks: int32 [8, 2, 2, 1], P(('clip', 'tm'), 'band'), parts along dimension 0, may hold values from 0 to 1
Outputs:
- attended: bfloat16 [8, 2, 256, 1536], P(('clip', 'tm'), 'band', None, 'head'), parts along dimension 0
There are 2 independent parts, one for each index of `clip`. A program takes and returns all parts, laid end to end along the dimension named above; each array names one. Nothing has to cross between parts.
Inputs may be any that keep to these rules, and one draw needn't show every extreme that they name: `adj_mask`: for each slab, band and direction exactly 1 of the 2 entries are 1.
All inputs are finite; a program needn't handle non-finite values.
Results may differ from a plain program's by a relative error of at most 0.0043.
Values may be sent and summed in bfloat16 or wider, within the bound.
A program may use at most 64 MiB of HBM per device.

v0:
```python
import math

import jax
import jax.numpy as jnp
from jax import lax
from jax.sharding import PartitionSpec as P

BLK = 128
BSEL = 1
HD = 128


masked_score = -1e30


def with_halo(array, sides, width):
    for axis, dim in sides:
        devices, length = (lax.axis_size(axis), array.shape[dim])
        up = [(i, (i + 1) % devices) for i in range(devices - 1)]
        down = [(j, i) for i, j in up]
        last = lax.slice_in_dim(array, length - width, length, axis=dim)
        first = lax.slice_in_dim(array, 0, width, axis=dim)
        before = lax.ppermute(last, axis, up)
        after = lax.ppermute(first, axis, down)
        array = jnp.concatenate([before, array, after], axis=dim)
    return array


def from_behind(value, axis, steps):
    count = lax.axis_size(axis)
    first, last = (max(0, -steps), min(count, count - steps))
    return lax.ppermute(value, axis, [(source, source + steps) for source in range(first, last)])


def attend(query_heads, key_rows, value_rows, bias, head_count):
    length = key_rows.shape[0]
    key_heads = key_rows.reshape(length, head_count, HD)
    value_heads = value_rows.reshape(length, head_count, HD)
    scores = (
        jnp.einsum("qhd,khd->hqk", query_heads, key_heads, preferred_element_type=jnp.float32)
        * (1.0 / math.sqrt(HD))
        + bias
    )
    maxima = jnp.max(scores, axis=2)
    weights = jnp.exp(scores - maxima[:, :, None])
    totals = jnp.sum(weights, axis=2)
    output = jnp.einsum(
        "hqk,khd->qhd",
        weights.astype(jnp.bfloat16),
        value_heads,
        preferred_element_type=jnp.float32,
    )
    return (maxima, totals, output)


def combine_sources(pieces):
    maxima = jnp.stack([piece[0] for piece in pieces])
    largest = jnp.max(maxima, axis=0)
    factors = jnp.exp(maxima - largest)
    numerator = factors[0].T[:, :, None] * pieces[0][2]
    for number in range(1, len(pieces)):
        numerator = numerator + factors[number].T[:, :, None] * pieces[number][2]
    denominator = jnp.sum(factors * jnp.stack([piece[1] for piece in pieces]), axis=0)
    return numerator / denominator.T[:, :, None]


def block_bias(mask_row, valid):
    return jnp.where(jnp.repeat(mask_row == 1, BLK) & valid, 0.0, masked_score).astype(jnp.float32)


def edge_bias(length, valid):
    return jnp.where(
        valid, jnp.zeros((length,), jnp.float32), jnp.full((length,), masked_score, jnp.float32)
    )


def per_device(queries, keys, values, adj_mask, border_blocks):
    row_count = queries.shape[2]
    feature_width = queries.shape[3]
    head_count = feature_width // HD
    blocks = row_count // BLK
    query_heads = queries[0, 0].reshape(row_count, head_count, HD)
    key_rows = keys[0, 0]
    value_rows = values[0, 0]
    slab_mask = adj_mask[0, 0]
    border_pick = border_blocks[0, 0]
    slab_index = lax.axis_index("tm")
    slab_count = lax.axis_size("tm")
    band_index = lax.axis_index("band")
    band_count = lax.axis_size("band")
    key_blocks = key_rows.reshape(blocks, BLK, feature_width)
    value_blocks = value_rows.reshape(blocks, BLK, feature_width)
    border_order = border_pick.reshape(-1)
    outgoing = jnp.stack(
        [
            jnp.take(key_blocks, border_order, axis=0).reshape(-1, feature_width),
            jnp.take(value_blocks, border_order, axis=0).reshape(-1, feature_width),
        ]
    )
    rim_rows = BSEL * BLK
    widened = with_halo(outgoing, (("band", 1),), rim_rows)
    own_piece = attend(
        query_heads, key_rows, value_rows, jnp.zeros((row_count,), jnp.float32), head_count
    )
    prev_keys, prev_values, prev_mask = from_behind((key_rows, value_rows, slab_mask[0]), "tm", 1)
    next_keys, next_values, next_mask = from_behind((key_rows, value_rows, slab_mask[1]), "tm", -1)
    prev_bias = block_bias(prev_mask, slab_index > 0)
    next_bias = block_bias(next_mask, slab_index < slab_count - 1)
    prev_piece = attend(query_heads, prev_keys, prev_values, prev_bias, head_count)
    next_piece = attend(query_heads, next_keys, next_values, next_bias, head_count)
    lower_piece = attend(
        query_heads,
        widened[0, :rim_rows],
        widened[1, :rim_rows],
        edge_bias(rim_rows, band_index > 0),
        head_count,
    )
    upper_piece = attend(
        query_heads,
        widened[0, -rim_rows:],
        widened[1, -rim_rows:],
        edge_bias(rim_rows, band_index < band_count - 1),
        head_count,
    )
    merged = combine_sources([own_piece, prev_piece, next_piece, lower_piece, upper_piece])
    return merged.reshape(row_count, feature_width).astype(jnp.bfloat16)[None, None]


def solution(mesh):
    placed = (
        P(("clip", "tm"), "band", None, "head"),
        P(("clip", "tm"), "band", None, "head"),
        P(("clip", "tm"), "band", None, "head"),
        P(("clip", "tm"), "band", None, None),
        P(("clip", "tm"), "band", None, None),
    )
    return jax.shard_map(
        per_device,
        mesh=mesh,
        in_specs=placed,
        out_specs=P(("clip", "tm"), "band", None, "head"),
        check_vma=False,
    )
```

profile of v0, /device:TPU:0, one launch (start us, length us, event | category | flops | bytes accessed | tf_op | source)
XLA Modules:
  0.0 61.2 jit_solution(8620650550110630350)
XLA Ops:
  0.0 2.0 %copy.46 = bf16[1,1,256,768]{2,3,1,0:T(8,128)(2,1)} copy(bf16[1,1,256,768]{3,2,1,0:T(8,128)(2,1)} %param.8) | data formatting | bytes 786432 | tf_op args[1]
  2.0 5.0 %collective-permute-start = (bf16[256,768]{0,1:T(8,128)(2,1)}, bf16[256,768]{0,1:T(8,128)(2,1)S(1)}, u32[]{:S(2)}, u32[]{:S(2)}) collective-permute-start(bf16[256,768]{0,1:T(8,128)(2,1)} %bitcast.3), channel_id=1, source_target_pairs={{0,4},{4,8},{8,12},{1,5},{5,9},{9,13},{2,6},{6,10},{10,14},{3,7},{... | collective-permute-start | bytes 1179656 | tf_op jit(solution)/shard_map/ppermute | solution.py:32
  7.0 1.3 %collective-permute-start.2 = (bf16[256,768]{0,1:T(8,128)(2,1)}, bf16[256,768]{0,1:T(8,128)(2,1)}, u32[]{:S(2)}, u32[]{:S(2)}) collective-permute-start(bf16[256,768]{0,1:T(8,128)(2,1)} %bitcast.3), channel_id=1, source_target_pairs={{4,0},{8,4},{12,8},{5,1},{9,5},{13,9},{6,2},{10,6},{14,10},{7,3},{... | collective-permute-start | bytes 1179656 | tf_op jit(solution)/shard_map/ppermute | solution.py:32
  8.3 1.3 %collective-permute-start.7 = (bf16[256,768]{1,0:T(8,128)(2,1)}, bf16[256,768]{1,0:T(8,128)(2,1)}, u32[]{:S(2)}, u32[]{:S(2)}) collective-permute-start(bf16[256,768]{1,0:T(8,128)(2,1)} %bitcast.128), channel_id=1, source_target_pairs={{4,0},{8,4},{12,8},{5,1},{9,5},{13,9},{6,2},{10,6},{14,10},{7,3},{... | collective-permute-start | bytes 1179656 | tf_op jit(solution)/shard_map/ppermute | solution.py:32
  9.6 5.9 %collective-permute-start.6 = (bf16[256,768]{1,0:T(8,128)(2,1)}, bf16[256,768]{1,0:T(8,128)(2,1)}, u32[]{:S(2)}, u32[]{:S(2)}) collective-permute-start(bf16[256,768]{1,0:T(8,128)(2,1)} %bitcast.129), channel_id=1, source_target_pairs={{0,4},{4,8},{8,12},{1,5},{5,9},{9,13},{2,6},{6,10},{10,14},{3,7},{... | collective-permute-start | bytes 1179656 | tf_op jit(solution)/shard_map/ppermute | solution.py:32
  15.5 0.8 %slice_bitcast_fusion.5 = (s32[2]{0:T(128)S(1)}, s32[2]{0:T(128)S(1)}) fusion(s32[1,1,2,2]{3,2,1,0:T(2,128)} %param.10), kind=kLoop, calls=%fused_computation.76 | loop fusion | bytes 32 | tf_op jit(solution)/shard_map/squeeze | solution.py:106
  16.3 3.8 %collective-permute-start.1 = (s32[2]{0:T(128)S(1)}, s32[2]{0:T(128)}, u32[]{:S(2)}, u32[]{:S(2)}) collective-permute-start(s32[2]{0:T(128)S(1)} %get-tuple-element.20), channel_id=1, source_target_pairs={{0,4},{4,8},{8,12},{1,5},{5,9},{9,13},{2,6},{6,10},{10,14},{3,7},{... | collective-permute-start | bytes 32 | tf_op jit(solution)/shard_map/ppermute | solution.py:32
  20.0 0.7 %compare_select_fusion = s32[2]{0:T(128)S(1)} fusion(s32[1,1,2,1]{2,3,1,0:T(1,128)} %param.11), kind=kLoop, calls=%fused_computation.72 | loop fusion | flops 6 | bytes 16 | tf_op jit(solution)/shard_map/jit(_take)/jit(_where)/select_n | solution.py:96
  20.7 0.7 %compare_and_fusion = pred[2]{0:T(512)(128)(4,1)S(1)} fusion(s32[1,1,2,1]{2,3,1,0:T(1,128)} %param.11), kind=kLoop, calls=%fused_computation.73 | loop fusion | flops 12 | bytes 10 | tf_op jit(solution)/shard_map/jit(_take)/and | solution.py:96
  21.3 1.9 %copy.60 = bf16[1,1,256,768]{2,3,1,0:T(8,128)(2,1)} copy(bf16[1,1,256,768]{3,2,1,0:T(8,128)(2,1)} %param.9) | data formatting | bytes 786432 | tf_op args[2]
  23.3 0.0 copy-done.3
  23.3 0.6 gather_fusion
  23.9 0.0 copy-done.4
  23.9 0.6 gather_fusion.1
  24.5 0.0 copy-start.7
  24.5 0.1 broadcast_select_fusion.1
  24.6 0.2 copy.54
  24.8 0.2 copy.55
  25.0 0.5 copy-done.7
  25.5 0.2 copy.45
  25.6 1.4 %fusion.39 = (f32[6,256]{1,0:T(8,128)S(1)}, f32[6,256,256]{1,2,0:T(8,128)S(1)}) fusion(bf16[256,6,128]{0,2,1:T(8,128)(2,1)S(1)} %bitcast.122, bf16[256,6,128]{0,2,1:T(8,128)(2,1)} %bitcast.1), kind=kOutput, calls=%fused_computation.83 | convolution fusion | flops 101448192 | bytes 2365440 | tf_op jit(solution)/shard_map/qhd,khd->hqk/dot_general | solution.py:40
  27.1 0.6 constant_dynamic-update-slice_fusion.4
  27.7 0.2 fusion
  27.9 0.1 fusion.33
  28.0 0.0 copy-start.12
  28.0 0.0 collective-permute-done.1
  28.1 1.3 %collective-permute-start.3 = (s32[2]{0:T(128)S(1)}, s32[2]{0:T(128)S(1)}, u32[]{:S(2)}, u32[]{:S(2)}) collective-permute-start(s32[2]{0:T(128)S(1)} %get-tuple-element.19), channel_id=1, source_target_pairs={{4,0},{8,4},{12,8},{5,1},{9,5},{13,9},{6,2},{10,6},{14,10},{7,3},{... | collective-permute-start | bytes 32 | tf_op jit(solution)/shard_map/ppermute | solution.py:32
  29.4 0.7 %and_select_fusion.1 = f32[2]{0:T(128)S(1)} fusion(s32[2]{0:T(128)} %collective-permute-done.1, pred[]{:T(512)S(6)} %gt.6), kind=kLoop, calls=%fused_computation.75 | loop fusion | flops 6 | bytes 17 | tf_op jit(solution)/shard_map/jit(_where)/select_n | solution.py:68
  30.0 0.1 broadcast_bitcast_fusion.1
  30.1 3.4 %collective-permute-done.3 = s32[2]{0:T(128)S(1)} collective-permute-done((s32[2]{0:T(128)S(1)}, s32[2]{0:T(128)S(1)}, u32[]{:S(2)}, u32[]{:S(2)}) %collective-permute-start.3) | collective-permute-done | bytes 40 | tf_op jit(solution)/shard_map/ppermute | solution.py:32
  33.5 1.3 %collective-permute-start.5 = (bf16[2,128,768]{1,2,0:T(8,128)(2,1)S(1)}, bf16[2,128,768]{1,2,0:T(8,128)(2,1)S(1)}, u32[]{:S(2)}, u32[]{:S(2)}) collective-permute-start(bf16[2,128,768]{1,2,0:T(8,128)(2,1)S(1)} %get-tuple-element.9), channel_id=1, source_target_pairs={{2,0},{3,1},{6,4},{7,5},{10,8},{11,9},{14,12},{15,13},{18,16},{19,... | collective-permute-start | bytes 1179656 | tf_op jit(solution)/shard_map/ppermute | solution.py:24
  34.8 0.1 broadcast_bitcast_fusion
  34.9 0.0 collective-permute-done
  34.9 4.6 %collective-permute-start.4 = (bf16[2,128,768]{1,2,0:T(8,128)(2,1)S(1)}, bf16[2,128,768]{1,2,0:T(8,128)(2,1)S(1)}, u32[]{:S(2)}, u32[]{:S(2)}) collective-permute-start(bf16[2,128,768]{1,2,0:T(8,128)(2,1)S(1)} %get-tuple-element.8), channel_id=1, source_target_pairs={{0,2},{1,3},{4,6},{5,7},{8,10},{9,11},{12,14},{13,15},{16,18},{17,... | collective-permute-start | bytes 1179656 | tf_op jit(solution)/shard_map/ppermute | solution.py:23
  39.5 0.0 copy-done.8
  39.5 1.4 %fusion.40 = (f32[6,256]{1,0:T(8,128)S(1)}, f32[6,256,256]{1,2,0:T(8,128)S(1)}) fusion(f32[256]{0:T(256)S(1)} %broadcast_bitcast_fusion.1, bf16[256,6,128]{0,2,1:T(8,128)(2,1)S(1)} %bitcast.123, bf16[256,6,128]{0,2,1:T(8,128)(2,1)} %bitcast.141), kind=kOutput, calls=%fused_computation.84 | convolution fusion | flops 101841408 | bytes 2366464 | tf_op jit(solution)/shard_map/qhd,khd->hqk/dot_general | solution.py:40
  40.9 0.0 collective-permute-done.2
  41.0 1.4 %fusion.41 = (f32[6,256]{1,0:T(8,128)S(1)}, f32[6,256,256]{1,2,0:T(8,128)S(1)}) fusion(f32[256]{0:T(256)S(1)} %broadcast_bitcast_fusion, bf16[256,6,128]{0,2,1:T(8,128)(2,1)S(1)} %bitcast.124, bf16[256,6,128]{0,2,1:T(8,128)(2,1)} %bitcast.8), kind=kOutput, calls=%fused_computation.85 | convolution fusion | flops 101841408 | bytes 2366464 | tf_op jit(solution)/shard_map/qhd,khd->hqk/dot_general | solution.py:40
  42.4 0.2 fusion.2
  42.6 2.3 %collective-permute-done.4 = bf16[2,128,768]{1,2,0:T(8,128)(2,1)S(1)} collective-permute-done((bf16[2,128,768]{1,2,0:T(8,128)(2,1)S(1)}, bf16[2,128,768]{1,2,0:T(8,128)(2,1)S(1)}, u32[]{:S(2)}, u32[]{:S(2)}) %collective-permute-start.4) | collective-permute-done | bytes 393248 | tf_op jit(solution)/shard_map/ppermute | solution.py:23
  45.0 0.7 %fusion.36 = (bf16[1,128,768]{1,2,0:T(8,128)(2,1)}, bf16[1,128,768]{1,2,0:T(8,128)(2,1)S(1)}) fusion(bf16[2,128,768]{1,2,0:T(8,128)(2,1)S(1)} %collective-permute-done.4), kind=kLoop, calls=%fused_computation.80 | loop fusion | bytes 786432 | tf_op jit(solution)/shard_map/slice | solution.py:114
  45.7 0.3 fusion.42
  46.0 0.8 %copy-done.1 = f32[6,256,128]{1,2,0:T(8,128)} copy-done((f32[6,256,128]{1,2,0:T(8,128)}, f32[6,256,128]{1,2,0:T(8,128)S(1)}, u32[]{:S(2)}) %copy-start.1) | copy-done | bytes 786456
  46.9 0.1 fusion.27
  47.0 0.2 fusion.4
  47.3 0.0 collective-permute-done.5
  47.3 0.3 fusion.38
  47.7 0.1 fusion.29
  47.9 0.6 multiply_reduce_fusion
  48.5 0.6 %slice_bitcast_fusion.3 = (f32[256,6]{0,1:T(8,128)}, f32[256,6]{0,1:T(8,128)S(1)}, f32[256,6]{0,1:T(8,128)}, f32[256,6]{0,1:T(8,128)}, f32[256,6]{0,1:T(8,128)}) fusion(f32[5,6,256]{2,1,0:T(8,128)S(1)} %get-tuple-element.7), kind=kLoop, calls=%fused_computation.68 | loop fusion | bytes 61440 | tf_op jit(solution)/shard_map/transpose | solution.py:62
  49.1 1.2 %fusion.14 = f32[256,6,128]{0,2,1:T(8,128)} fusion(bf16[128,6,128]{0,2,1:T(8,128)(2,1)S(1)} %bitcast.138, f32[6,256,128]{1,2,0:T(8,128)S(1)} %get-tuple-element.24, f32[6,256]{1,0:T(8,128)S(1)} %get-tuple-element.23, f32[256,6]{0,1:T(8,128)S(1)} %get-tuple-element.15), kind=kOutput, calls=%fused_computation.26 | convolution fusion | flops 50921472 | bytes 1781760 | tf_op jit(solution)/shard_map/hqk,khd->qhd/dot_general | solution.py:47
  50.3 0.0 collective-permute-done.7
  50.3 1.2 %copy.64 = bf16[256,768]{0,1:T(8,128)(2,1)S(1)} copy(bf16[256,768]{1,0:T(8,128)(2,1)} %collective-permute-done.7) | data formatting | bytes 786432 | tf_op jit(solution)/shard_map/ppermute | solution.py:32
  51.5 0.0 copy-start.6
  51.5 2.8 %fusion.13 = f32[256,6,128]{0,2,1:T(8,128)} fusion(bf16[256,6,128]{0,2,1:T(8,128)(2,1)S(1)} %bitcast.134, f32[6,256,256]{1,2,0:T(8,128)} %copy-done, f32[6,256]{1,0:T(8,128)} %copy-done.9, f32[256,6]{0,1:T(8,128)} %get-tuple-element.17), kind=kOutput, calls=%fused_computation.24 | convolution fusion | flops 101646336 | bytes 2764800 | tf_op jit(solution)/shard_map/hqk,khd->qhd/dot_general | solution.py:47
  54.3 0.0 copy-done.2
  54.3 1.2 %fusion.15 = f32[256,6,128]{0,2,1:T(8,128)} fusion(bf16[128,6,128]{0,2,1:T(8,128)(2,1)S(1)} %bitcast.137, f32[6,256,128]{1,2,0:T(8,128)S(1)} %copy-done.2, f32[6,256]{1,0:T(8,128)S(1)} %copy-done.11, f32[256,6]{0,1:T(8,128)S(1)} %copy-done.16), kind=kOutput, calls=%fused_computation.28 | convolution fusion | flops 50921472 | bytes 1781760 | tf_op jit(solution)/shard_map/hqk,khd->qhd/dot_general | solution.py:47
  55.5 1.3 %fusion.6 = f32[256,6,128]{0,2,1:T(8,128)} fusion(bf16[256,6,128]{0,2,1:T(8,128)(2,1)S(1)} %bitcast.133, f32[6,256,256]{1,2,0:T(8,128)S(1)} %get-tuple-element.26, f32[6,256]{1,0:T(8,128)S(1)} %get-tuple-element.25, f32[256,6]{0,1:T(8,128)S(1)} %copy-done.15), kind=kOutput, calls=%fused_computation.17 | convolution fusion | flops 101646336 | bytes 2764800 | tf_op jit(solution)/shard_map/hqk,khd->qhd/dot_general | solution.py:47
  56.8 0.0 collective-permute-done.6
  56.8 1.2 %copy.62 = bf16[256,768]{0,1:T(8,128)(2,1)S(1)} copy(bf16[256,768]{1,0:T(8,128)(2,1)} %collective-permute-done.6) | data formatting | bytes 786432 | tf_op jit(solution)/shard_map/ppermute | solution.py:32
  58.0 0.0 copy-done.13
  58.0 0.0 copy-done.14
  58.0 2.3 %fusion.20 = bf16[256,6,128]{0,2,1:T(8,128)(2,1)S(1)} fusion(f32[256,6,128]{0,2,1:T(8,128)} %fusion.14, f32[256,6,128]{0,2,1:T(8,128)} %fusion.15, f32[256,6,128]{0,2,1:T(8,128)} %fusion.13, f32[256,6,128]{0,2,1:T(8,128)} %fusion.6, bf16[256,6,128]{0,2,1:T(8,128)(2,1)S(1)} %bitcast.135, f32[6,256,256]{1,2,0:T(8,128)S(1)} %get-tuple-element.28, ...), kind=kOutput, calls=%fused_computation.35 | convolution fusion | flops 102825984 | bytes 5523456 | tf_op jit(solution)/shard_map/hqk,khd->qhd/dot_general | solution.py:47
  60.3 0.9 %copy.68 = bf16[1,1,256,768]{3,2,1,0:T(8,128)(2,1)} copy(bf16[1,1,256,768]{2,3,1,0:T(8,128)(2,1)S(1)} %bitcast.136) | data formatting | bytes 786432 | tf_op jit(solution)/shard_map/convert_element_type | solution.py:126
  (35 shorter events, 0.1 us)
Async XLA Ops:
  0.0 23.3 %copy-start.3 = (bf16[1,1,256,768]{3,2,1,0:T(8,128)(2,1)S(1)}, bf16[1,1,256,768]{3,2,1,0:T(8,128)(2,1)}, u32[]{:S(2)}) copy-start(bf16[1,1,256,768]{3,2,1,0:T(8,128)(2,1)} %param.8) | copy-start | bytes 1179652
  0.0 23.9 %copy-start.4 = (bf16[1,1,256,768]{3,2,1,0:T(8,128)(2,1)S(1)}, bf16[1,1,256,768]{3,2,1,0:T(8,128)(2,1)}, u32[]{:S(2)}) copy-start(bf16[1,1,256,768]{3,2,1,0:T(8,128)(2,1)} %param.9) | copy-start | bytes 1179652
  2.0 32.9 %collective-permute-start = (bf16[256,768]{0,1:T(8,128)(2,1)}, bf16[256,768]{0,1:T(8,128)(2,1)S(1)}, u32[]{:S(2)}, u32[]{:S(2)}) collective-permute-start(bf16[256,768]{0,1:T(8,128)(2,1)} %bitcast.3), channel_id=1, source_target_pairs={{0,4},{4,8},{8,12},{1,5},{5,9},{9,13},{2,6},{6,10},{10,14},{3,7},{... | collective-permute-start | bytes 1179656 | tf_op jit(solution)/shard_map/ppermute | solution.py:32
  7.0 34.0 %collective-permute-start.2 = (bf16[256,768]{0,1:T(8,128)(2,1)}, bf16[256,768]{0,1:T(8,128)(2,1)}, u32[]{:S(2)}, u32[]{:S(2)}) collective-permute-start(bf16[256,768]{0,1:T(8,128)(2,1)} %bitcast.3), channel_id=1, source_target_pairs={{4,0},{8,4},{12,8},{5,1},{9,5},{13,9},{6,2},{10,6},{14,10},{7,3},{... | collective-permute-start | bytes 1179656 | tf_op jit(solution)/shard_map/ppermute | solution.py:32
  8.3 42.0 %collective-permute-start.7 = (bf16[256,768]{1,0:T(8,128)(2,1)}, bf16[256,768]{1,0:T(8,128)(2,1)}, u32[]{:S(2)}, u32[]{:S(2)}) collective-permute-start(bf16[256,768]{1,0:T(8,128)(2,1)} %bitcast.128), channel_id=1, source_target_pairs={{4,0},{8,4},{12,8},{5,1},{9,5},{13,9},{6,2},{10,6},{14,10},{7,3},{... | collective-permute-start | bytes 1179656 | tf_op jit(solution)/shard_map/ppermute | solution.py:32
  9.6 47.2 %collective-permute-start.6 = (bf16[256,768]{1,0:T(8,128)(2,1)}, bf16[256,768]{1,0:T(8,128)(2,1)}, u32[]{:S(2)}, u32[]{:S(2)}) collective-permute-start(bf16[256,768]{1,0:T(8,128)(2,1)} %bitcast.129), channel_id=1, source_target_pairs={{0,4},{4,8},{8,12},{1,5},{5,9},{9,13},{2,6},{6,10},{10,14},{3,7},{... | collective-permute-start | bytes 1179656 | tf_op jit(solution)/shard_map/ppermute | solution.py:32
  16.3 11.8 %collective-permute-start.1 = (s32[2]{0:T(128)S(1)}, s32[2]{0:T(128)}, u32[]{:S(2)}, u32[]{:S(2)}) collective-permute-start(s32[2]{0:T(128)S(1)} %get-tuple-element.20), channel_id=1, source_target_pairs={{0,4},{4,8},{8,12},{1,5},{5,9},{9,13},{2,6},{6,10},{10,14},{3,7},{... | collective-permute-start | bytes 32 | tf_op jit(solution)/shard_map/ppermute | solution.py:32
  24.5 1.0 %copy-start.7 = (bf16[1,1,256,768]{3,2,1,0:T(8,128)(2,1)S(1)}, bf16[1,1,256,768]{3,2,1,0:T(8,128)(2,1)}, u32[]{:S(2)}) copy-start(bf16[1,1,256,768]{3,2,1,0:T(8,128)(2,1)} %param.7) | copy-start | bytes 1179652
  28.0 12.9 %copy-start.12 = (f32[5,6,256]{2,1,0:T(8,128)S(1)}, f32[5,6,256]{2,1,0:T(8,128)}, u32[]{:S(2)}) copy-start(f32[5,6,256]{2,1,0:T(8,128)} %constant_dynamic-update-slice_fusion.4) | copy-start | bytes 92164
  28.1 5.5 %collective-permute-start.3 = (s32[2]{0:T(128)S(1)}, s32[2]{0:T(128)S(1)}, u32[]{:S(2)}, u32[]{:S(2)}) collective-permute-start(s32[2]{0:T(128)S(1)} %get-tuple-element.19), channel_id=1, source_target_pairs={{4,0},{8,4},{12,8},{5,1},{9,5},{13,9},{6,2},{10,6},{14,10},{7,3},{... | collective-permute-start | bytes 32 | tf_op jit(solution)/shard_map/ppermute | solution.py:32
  33.5 13.7 %collective-permute-start.5 = (bf16[2,128,768]{1,2,0:T(8,128)(2,1)S(1)}, bf16[2,128,768]{1,2,0:T(8,128)(2,1)S(1)}, u32[]{:S(2)}, u32[]{:S(2)}) collective-permute-start(bf16[2,128,768]{1,2,0:T(8,128)(2,1)S(1)} %get-tuple-element.9), channel_id=1, source_target_pairs={{2,0},{3,1},{6,4},{7,5},{10,8},{11,9},{14,12},{15,13},{18,16},{19,... | collective-permute-start | bytes 1179656 | tf_op jit(solution)/shard_map/ppermute | solution.py:24
  34.9 4.6 %copy-start.8 = (bf16[256,768]{0,1:T(8,128)(2,1)}, bf16[256,768]{0,1:T(8,128)(2,1)S(1)}, u32[]{:S(2)}) copy-start(bf16[256,768]{0,1:T(8,128)(2,1)S(1)} %collective-permute-done) | copy-start | bytes 1179652
  34.9 10.1 %collective-permute-start.4 = (bf16[2,128,768]{1,2,0:T(8,128)(2,1)S(1)}, bf16[2,128,768]{1,2,0:T(8,128)(2,1)S(1)}, u32[]{:S(2)}, u32[]{:S(2)}) collective-permute-start(bf16[2,128,768]{1,2,0:T(8,128)(2,1)S(1)} %get-tuple-element.8), channel_id=1, source_target_pairs={{0,2},{1,3},{4,6},{5,7},{8,10},{9,11},{12,14},{13,15},{16,18},{17,... | collective-permute-start | bytes 1179656 | tf_op jit(solution)/shard_map/ppermute | solution.py:23
  42.4 4.6 %copy-start = (f32[6,256,256]{1,2,0:T(8,128)}, f32[6,256,256]{1,2,0:T(8,128)S(1)}, u32[]{:S(2)}) copy-start(f32[6,256,256]{1,2,0:T(8,128)S(1)} %get-tuple-element.30) | copy-start | bytes 4718596
  42.4 5.3 %copy-start.9 = (f32[6,256]{1,0:T(8,128)}, f32[6,256]{1,0:T(8,128)S(1)}, u32[]{:S(2)}) copy-start(f32[6,256]{1,0:T(8,128)S(1)} %get-tuple-element.29) | copy-start | bytes 18436
  46.0 0.9 %copy-start.1 = (f32[6,256,128]{1,2,0:T(8,128)}, f32[6,256,128]{1,2,0:T(8,128)S(1)}, u32[]{:S(2)}) copy-start(f32[6,256,128]{1,2,0:T(8,128)S(1)} %get-tuple-element.32) | copy-start | bytes 2359300
  46.0 1.6 %copy-start.10 = (f32[6,256]{1,0:T(8,128)}, f32[6,256]{1,0:T(8,128)S(1)}, u32[]{:S(2)}) copy-start(f32[6,256]{1,0:T(8,128)S(1)} %get-tuple-element.31) | copy-start | bytes 18436
  51.4 2.8 %copy-start.2 = (f32[6,256,128]{1,2,0:T(8,128)S(1)}, f32[6,256,128]{1,2,0:T(8,128)}, u32[]{:S(2)}) copy-start(f32[6,256,128]{1,2,0:T(8,128)} %copy-done.1) | copy-start | bytes 2359300
  51.5 2.8 %copy-start.6 = (bf16[1,128,768]{1,2,0:T(8,128)(2,1)S(1)}, bf16[1,128,768]{1,2,0:T(8,128)(2,1)}, u32[]{:S(2)}) copy-start(bf16[1,128,768]{1,2,0:T(8,128)(2,1)} %get-tuple-element.10) | copy-start | bytes 589828
  51.5 2.8 %copy-start.11 = (f32[6,256]{1,0:T(8,128)S(1)}, f32[6,256]{1,0:T(8,128)}, u32[]{:S(2)}) copy-start(f32[6,256]{1,0:T(8,128)} %copy-done.10) | copy-start | bytes 18436
  51.5 2.8 %copy-start.16 = (f32[256,6]{0,1:T(8,128)S(1)}, f32[256,6]{0,1:T(8,128)}, u32[]{:S(2)}) copy-start(f32[256,6]{0,1:T(8,128)} %get-tuple-element.16) | copy-start | bytes 18436
  54.3 1.2 %copy-start.5 = (bf16[1,1,256,768]{2,3,1,0:T(8,128)(2,1)S(1)}, bf16[1,1,256,768]{2,3,1,0:T(8,128)(2,1)}, u32[]{:S(2)}) copy-start(bf16[1,1,256,768]{2,3,1,0:T(8,128)(2,1)} %copy.60) | copy-start | bytes 1179652
  54.3 1.2 %copy-start.15 = (f32[256,6]{0,1:T(8,128)S(1)}, f32[256,6]{0,1:T(8,128)}, u32[]{:S(2)}) copy-start(f32[256,6]{0,1:T(8,128)} %get-tuple-element.18) | copy-start | bytes 18436
  55.5 2.5 %copy-start.13 = (f32[6,256]{1,0:T(8,128)S(1)}, f32[6,256]{1,0:T(8,128)}, u32[]{:S(2)}) copy-start(f32[6,256]{1,0:T(8,128)} %get-tuple-element.6) | copy-start | bytes 18436
  55.5 2.5 %copy-start.14 = (f32[256,6]{0,1:T(8,128)S(1)}, f32[256,6]{0,1:T(8,128)}, u32[]{:S(2)}) copy-start(f32[256,6]{0,1:T(8,128)} %get-tuple-element.14) | copy-start | bytes 18436
where the time goes:
time: 61.9 us; the launch traced here: 61.2 us
  starting transfers between devices  24.4 us (39%)
  matrix products  13.7 us (22%)
  local copies, waits for them, and re-layouts  13.1 us (21%)
  waiting for transfers between devices  5.75 us (9%)
  other arithmetic  3.83 us (6%)
    ppermute x6, starting transfers between devices, from_behind(): lax.ppermute(value, axis, [(source, source + steps) for source in range(f...  18.5 us
    dot_general x5, matrix products, attend(): jnp.einsum('hqk,khd->qhd', weights.astype(jnp.bfloat16), value_heads, pre...  8.76 us
    unnamed x45, local copies, waits for them, and re-layouts  6.11 us
    dot_general x5, matrix products, attend(): jnp.einsum('qhd,khd->hqk', query_heads, key_heads, preferred_element_type...  4.92 us
    ppermute x1, starting transfers between devices, with_halo(): before = lax.ppermute(last, axis, up)  4.58 us
    ppermute x6, waiting for transfers between devices, from_behind(): lax.ppermute(value, axis, [(source, source + steps) for source in range(f...  3.41 us
    ppermute x1, waiting for transfers between devices, with_halo(): before = lax.ppermute(last, axis, up)  2.33 us
    ppermute x2, local copies, waits for them, and re-layouts, from_behind(): lax.ppermute(value, axis, [(source, source + steps) for source in range(f...  2.33 us
  transfers between devices with their start and end apart: 8, of which 2 were waited for; matrix products, arithmetic and copies ran while one was open for 37% of the time, Pallas kernels for 0%

commit v1 on v0

v1 whole, which is shorter than its diff:
```python
import functools
import math

import jax
import jax.numpy as jnp
from jax import lax
from jax.experimental import pallas as pl
from jax.experimental.pallas import tpu as pltpu
from jax.sharding import PartitionSpec as P

BLK = 128
HD = 128
GROUP = 2

masked_score = -1e30
SCALE2 = math.log2(math.e) / math.sqrt(HD)
MESH = pl.DeviceIdType.MESH


def routes(slab_count, band_count):
    slab, band = lax.axis_index("tm"), lax.axis_index("band")
    found = []
    if slab_count > 1:
        found.append(({"tm": slab + 1}, slab < slab_count - 1, slab > 0, ("adj", 0)))
        found.append(({"tm": slab - 1}, slab > 0, slab < slab_count - 1, ("adj", 1)))
    if band_count == 2:
        found.append(({"band": 1 - band}, None, None, ("border", 1 - band)))
    elif band_count > 2:
        found.append(({"band": band + 1}, band < band_count - 1, band > 0, ("border", 1)))
        found.append(({"band": band - 1}, band > 0, band < band_count - 1, ("border", 0)))
    return found


def when(condition):
    return (lambda body: body()) if condition is None else pl.when(condition)


def weigh(query, key):
    scores = lax.dot_general(
        query, key, (((1,), (1,)), ((), ())), preferred_element_type=jnp.float32
    )
    return scores * SCALE2


def kernel(
    slab_count, band_count, q_hbm, k_hbm, v_hbm, adj_hbm, border_hbm, out_hbm,
    q_ref, k_ref, v_ref, adj_ref, border_ref, send_ref, recv_ref, acc_ref, weights_ref,
    gain_ref, out_ref, load_sem, store_sem, send_sem, recv_sem,
):
    plan = routes(slab_count, band_count)
    rows, width = q_ref.shape
    heads = width // HD
    groups = heads // GROUP

    barrier = pltpu.get_barrier_semaphore()
    for target, sends, _, _ in plan:
        @when(sends)
        def _():
            pl.semaphore_signal(barrier, inc=1, device_id=target, device_id_type=MESH)

    loads = []
    for number, (source, target) in enumerate(
        ((adj_hbm, adj_ref), (border_hbm, border_ref), (k_hbm, k_ref), (v_hbm, v_ref), (q_hbm, q_ref))
    ):
        copy = pltpu.make_async_copy(source, target, load_sem.at[number])
        copy.start()
        loads.append(copy)

    for slot, (_, _, comes, _) in enumerate(plan):
        if comes is not None:
            @pl.when(jnp.logical_not(comes))
            def _():
                recv_ref[slot] = jnp.zeros(recv_ref.shape[1:], recv_ref.dtype)

    loads[0].wait()
    loads[1].wait()
    starts = []
    for _, _, _, (kind, row) in plan:
        starts.append(adj_ref[row, 1] if kind == "adj" else border_ref[0, row])
    for part, (load, whole) in enumerate(((loads[2], k_ref), (loads[3], v_ref))):
        load.wait()
        for slot in range(len(plan)):
            for head in range(heads):
                send_ref[slot, part, head] = whole[
                    starts[slot], :, head * HD : (head + 1) * HD
                ]

    arrivals = sum(1 if comes is None else comes.astype(jnp.int32) for _, _, comes, _ in plan)
    pl.semaphore_wait(barrier, arrivals)

    def transfer(slot, part, group):
        at = (slot, part, pl.ds(group * GROUP, GROUP))
        return pltpu.make_async_remote_copy(
            src_ref=send_ref.at[at],
            dst_ref=recv_ref.at[at],
            send_sem=send_sem.at[slot, part, group],
            recv_sem=recv_sem.at[slot, part, group],
            device_id=plan[slot][0],
            device_id_type=MESH,
        )

    for part in range(2):
        for group in range(groups):
            for slot, (_, sends, _, _) in enumerate(plan):
                @when(sends)
                def _():
                    transfer(slot, part, group).start()

    loads[4].wait()
    own = []
    for head in range(heads):
        columns = slice(head * HD, (head + 1) * HD)
        scores = weigh(q_ref[:, columns], k_ref[:, :, columns].reshape(rows, HD))
        most = jnp.max(scores, axis=1, keepdims=True)
        weights = jnp.exp2(scores - most)
        total = jnp.sum(weights, axis=1, keepdims=True)
        acc_ref[head] = jnp.dot(
            weights.astype(jnp.bfloat16), v_ref[:, :, columns].reshape(rows, HD), preferred_element_type=jnp.float32
        )
        own.append((most, total))

    for group in range(groups):
        for slot, (_, _, comes, _) in enumerate(plan):
            @when(comes)
            def _():
                transfer(slot, 0, group).wait_recv()
        for head in range(group * GROUP, (group + 1) * GROUP):
            columns = slice(head * HD, (head + 1) * HD)
            pieces = [own[head]]
            for slot, (_, _, comes, _) in enumerate(plan):
                scores = weigh(q_ref[:, columns], recv_ref[slot, 0, head])
                if comes is not None:
                    scores = scores + jnp.where(comes, 0.0, masked_score).astype(jnp.float32)
                most = jnp.max(scores, axis=1, keepdims=True)
                weights = jnp.exp2(scores - most)
                total = jnp.sum(weights, axis=1, keepdims=True)
                weights_ref[head, slot] = weights.astype(jnp.bfloat16)
                pieces.append((most, total))
            largest = functools.reduce(jnp.maximum, [most for most, _ in pieces])
            factors = [jnp.exp2(most - largest) for most, _ in pieces]
            denominator = sum(factor * total for factor, (_, total) in zip(factors, pieces))
            acc_ref[head] = acc_ref[head] * (factors[0] / denominator)
            for slot in range(len(plan)):
                gain_ref[head, slot] = jnp.broadcast_to(
                    factors[slot + 1] / denominator, (rows, HD)
                )

    stores = []
    for group in range(groups):
        for slot, (_, _, comes, _) in enumerate(plan):
            @when(comes)
            def _():
                transfer(slot, 1, group).wait_recv()
        for head in range(group * GROUP, (group + 1) * GROUP):
            result = acc_ref[head]
            for slot in range(len(plan)):
                result = result + gain_ref[head, slot] * jnp.dot(
                    weights_ref[head, slot], recv_ref[slot, 1, head], preferred_element_type=jnp.float32
                )
            out_ref[:, head * HD : (head + 1) * HD] = result.astype(out_ref.dtype)
        columns = pl.ds(group * GROUP * HD, GROUP * HD)
        store = pltpu.make_async_copy(
            out_ref.at[:, columns], out_hbm.at[:, columns], store_sem.at[group]
        )
        store.start()
        stores.append(store)

    for part in range(2):
        for group in range(groups):
            for slot, (_, sends, _, _) in enumerate(plan):
                @when(sends)
                def _():
                    transfer(slot, part, group).wait_send()
    for store in stores:
        store.wait()


def per_device(queries, keys, values, adj_mask, border_blocks):
    rows, width = queries.shape[2:]
    heads = width // HD
    slab_count, band_count = lax.axis_size("tm"), lax.axis_size("band")
    sources = (2 if slab_count > 1 else 0) + min(band_count - 1, 2)
    assert rows == 2 * BLK and adj_mask.shape[3] == 2 and border_blocks.shape[3] == 1
    block_sems = pltpu.SemaphoreType.DMA((sources, 2, heads // GROUP))
    attended = pl.pallas_call(
        functools.partial(kernel, slab_count, band_count),
        out_shape=jax.ShapeDtypeStruct((rows, width), jnp.bfloat16),
        in_specs=[pl.BlockSpec(memory_space=pl.ANY)] * 5,
        out_specs=pl.BlockSpec(memory_space=pl.ANY),
        scratch_shapes=[
            pltpu.VMEM((rows, width), jnp.bfloat16),
            pltpu.VMEM((rows // BLK, BLK, width), jnp.bfloat16),
            pltpu.VMEM((rows // BLK, BLK, width), jnp.bfloat16),
            pltpu.SMEM(adj_mask.shape[2:], jnp.int32),
            pltpu.SMEM(border_blocks.shape[:1:-1], jnp.int32),
            pltpu.VMEM((sources, 2, heads, BLK, HD), jnp.bfloat16),
            pltpu.VMEM((sources, 2, heads, BLK, HD), jnp.bfloat16),
            pltpu.VMEM((heads, rows, HD), jnp.float32),
            pltpu.VMEM((heads, sources, rows, BLK), jnp.bfloat16),
            pltpu.VMEM((heads, sources, rows, HD), jnp.float32),
            pltpu.VMEM((rows, width), jnp.bfloat16),
            pltpu.SemaphoreType.DMA((5,)),
            pltpu.SemaphoreType.DMA((heads // GROUP,)),
            block_sems,
            block_sems,
        ],
        compiler_params=pltpu.CompilerParams(collective_id=0, has_side_effects=True),
        name="radial_attention",
    )(
        queries[0, 0],
        keys.reshape(rows // BLK, BLK, width),
        values.reshape(rows // BLK, BLK, width),
        adj_mask[0, 0], border_blocks[0, 0].T,
    )
    return attended[None, None]


def solution(mesh):
    placed = (
        P(("clip", "tm"), "band", None, "head"),
        P(("clip", "tm"), "band", None, "head"),
        P(("clip", "tm"), "band", None, "head"),
        P(("clip", "tm"), "band", None, None),
        P(("clip", "tm"), "band", None, None),
    )
    return jax.shard_map(
        per_device,
        mesh=mesh,
        in_specs=placed,
        out_specs=P(("clip", "tm"), "band", None, "head"),
        check_vma=False,
    )
```

time: 61.9 us -> 16.7 us (0.27)
  starting transfers between devices: 24.4 us -> 0 us
  Pallas kernels: 0 us -> 14.8 us
  matrix products: 13.7 us -> 0 us
  local copies, waits for them, and re-layouts: 13.1 us -> 1.77 us
  waiting for transfers between devices: 5.75 us -> 0 us
  other arithmetic: 3.83 us -> 0 us
    ppermute x8 -> x0, starting transfers between devices: 24.4 us -> none  [the longest x6 18.5 us: from_behind(): lax.ppermute(value, axis, [(source, source + steps) for source in range(f...]
    pallas_call x0 -> x1, Pallas kernels: none -> 14.8 us  [per_device(): pl.pallas_call(functools.partial(kernel, slab_count, band_count), out_sha...]
    dot_general x10 -> x0, matrix products: 13.7 us -> none  [the longest x5 8.76 us: attend(): jnp.einsum('hqk,khd->qhd', weights.astype(jnp.bfloat16), value_heads, pre...]
    ppermute x8 -> x0, waiting for transfers between devices: 5.75 us -> none  [the longest x6 3.41 us: from_behind(): lax.ppermute(value, axis, [(source, source + steps) for source in range(f...]
    unnamed x45 -> x1, local copies, waits for them, and re-layouts: 6.11 us -> 1.77 us
    ppermute x2 -> x0, local copies, waits for them, and re-layouts: 2.33 us -> none  [from_behind(): lax.ppermute(value, axis, [(source, source + steps) for source in range(f...]
    reduce_sum x6 -> x0, other arithmetic: 1.52 us -> none  [the longest x5 0.91 us: attend(): totals = jnp.sum(weights, axis=2)]
    select_n x4 -> x0, other arithmetic: 1.49 us -> none  [the longest x2 0.8 us: per_device(): jnp.take(key_blocks, border_order, axis=0).reshape(-1, feature_width)]
  transfers between devices with their start and end apart: 8 -> 0, of which waited for: 2 -> 0; matrix products, arithmetic and copies ran while one was open for 37% -> 0% of each run, Pallas kernels for 0% -> 0%
where the time goes in v1:
time: 16.7 us; the launch traced here: 16.5 us
  Pallas kernels  14.8 us (89%)
  local copies, waits for them, and re-layouts  1.77 us (11%)
    pallas_call x1, Pallas kernels, per_device(): pl.pallas_call(functools.partial(kernel, slab_count, band_count), out_sha...  14.8 us
    unnamed x1, local copies, waits for them, and re-layouts  1.77 us

profile of v1, /device:TPU:0, one launch (start us, length us, event | category | flops | bytes accessed | tf_op | source)
XLA Modules:
  0.0 16.5 jit_solution(10385029747913331630)
XLA Ops:
  0.0 14.8 %radial_attention.1 = bf16[256,768]{1,0:T(8,128)(2,1)} custom-call(bf16[256,768]{1,0:T(8,128)(2,1)} %bitcast.7, bf16[2,128,768]{2,1,0:T(8,128)(2,1)} %bitcast.8, bf16[2,128,768]{2,1,0:T(8,128)(2,1)} %bitcast.9, s32[2,2]{1,0:T(2,128)} %bitcast.10, s32[1,2]{1,0:T(1,128)} %bitcast.11), custom_call_target="tpu_custom_call" | custom-call | tf_op jit(solution)/shard_map/radial_attention/pallas_call | solution.py:185
  14.8 1.8 %copy.7 = bf16[1,1,256,768]{3,2,1,0:T(8,128)(2,1)} copy(bf16[1,1,256,768]{3,2,1,0:T(8,128)(2,1)} %bitcast.6) | data formatting | bytes 786432

commit v2 on v1

--- a/solution.py
+++ b/solution.py
@@ -43,9 +43,9 @@
 
 
 def kernel(
-    slab_count, band_count, q_hbm, k_hbm, v_hbm, adj_hbm, border_hbm, out_hbm,
+    slab_count, band_count, q_hbm, k_hbm, v_hbm, adj_hbm, border_hbm, out_ref,
     q_ref, k_ref, v_ref, adj_ref, border_ref, send_ref, recv_ref, acc_ref, weights_ref,
-    gain_ref, out_ref, load_sem, store_sem, send_sem, recv_sem,
+    gain_ref, load_sem, send_sem, recv_sem,
 ):
     plan = routes(slab_count, band_count)
     rows, width = q_ref.shape
@@ -145,7 +145,6 @@
                     factors[slot + 1] / denominator, (rows, HD)
                 )
 
-    stores = []
     for group in range(groups):
         for slot, (_, _, comes, _) in enumerate(plan):
             @when(comes)
@@ -158,12 +157,6 @@
                     weights_ref[head, slot], recv_ref[slot, 1, head], preferred_element_type=jnp.float32
                 )
             out_ref[:, head * HD : (head + 1) * HD] = result.astype(out_ref.dtype)
-        columns = pl.ds(group * GROUP * HD, GROUP * HD)
-        store = pltpu.make_async_copy(
-            out_ref.at[:, columns], out_hbm.at[:, columns], store_sem.at[group]
-        )
-        store.start()
-        stores.append(store)
 
     for part in range(2):
         for group in range(groups):
@@ -171,8 +164,6 @@
                 @when(sends)
                 def _():
                     transfer(slot, part, group).wait_send()
-    for store in stores:
-        store.wait()
 
 
 def per_device(queries, keys, values, adj_mask, border_blocks):
@@ -184,9 +175,9 @@
     block_sems = pltpu.SemaphoreType.DMA((sources, 2, heads // GROUP))
     attended = pl.pallas_call(
         functools.partial(kernel, slab_count, band_count),
-        out_shape=jax.ShapeDtypeStruct((rows, width), jnp.bfloat16),
+        out_shape=pltpu.VMEM((rows, width), jnp.bfloat16),
         in_specs=[pl.BlockSpec(memory_space=pl.ANY)] * 5,
-        out_specs=pl.BlockSpec(memory_space=pl.ANY),
+        out_specs=pl.BlockSpec(memory_space=pltpu.VMEM),
         scratch_shapes=[
             pltpu.VMEM((rows, width), jnp.bfloat16),
             pltpu.VMEM((rows // BLK, BLK, width), jnp.bfloat16),
@@ -198,9 +189,7 @@
             pltpu.VMEM((heads, rows, HD), jnp.float32),
             pltpu.VMEM((heads, sources, rows, BLK), jnp.bfloat16),
             pltpu.VMEM((heads, sources, rows, HD), jnp.float32),
-            pltpu.VMEM((rows, width), jnp.bfloat16),
             pltpu.SemaphoreType.DMA((5,)),
-            pltpu.SemaphoreType.DMA((heads // GROUP,)),
             block_sems,
             block_sems,
         ],

time: 16.7 us -> 15 us (0.90)
  local copies, waits for them, and re-layouts: 1.77 us -> 0.75 us
  Pallas kernels: 14.8 us -> 14.1 us
    unnamed x1, local copies, waits for them, and re-layouts: 1.77 us -> 0.75 us
    pallas_call x1, Pallas kernels: 14.8 us -> 14.1 us  [per_device(): pl.pallas_call(functools.partial(kernel, slab_count, band_count), out_sha...]
where the time goes in v2:
time: 15 us; the launch traced here: 14.9 us
  Pallas kernels  14.1 us (94%)
  local copies, waits for them, and re-layouts  0.75 us (5%)
    pallas_call x1, Pallas kernels, per_device(): pl.pallas_call(functools.partial(kernel, slab_count, band_count), out_sha...  14.1 us
    unnamed x1, local copies, waits for them, and re-layouts  0.75 us

profile of v2, /device:TPU:0, one launch (start us, length us, event | category | flops | bytes accessed | tf_op | source)
XLA Modules:
  0.0 14.9 jit_solution(2828174348711579453)
XLA Ops:
  0.0 14.1 %radial_attention.1 = bf16[256,768]{1,0:T(8,128)(2,1)S(1)} custom-call(bf16[256,768]{1,0:T(8,128)(2,1)} %bitcast.7, bf16[2,128,768]{2,1,0:T(8,128)(2,1)} %bitcast.8, bf16[2,128,768]{2,1,0:T(8,128)(2,1)} %bitcast.9, s32[2,2]{1,0:T(2,128)} %bitcast.10, s32[1,2]{1,0:T(1,128)} %bitcast.11), custom_call_target="tpu_custom_call" | custom-call | tf_op jit(solution)/shard_map/radial_attention/pallas_call | solution.py:176
  14.1 0.7 %copy.7 = bf16[1,1,256,768]{3,2,1,0:T(8,128)(2,1)} copy(bf16[1,1,256,768]{3,2,1,0:T(8,128)(2,1)S(1)} %bitcast.6) | data formatting | bytes 786432

commit v3 on v2

--- a/solution.py
+++ b/solution.py
@@ -10,7 +10,6 @@
 
 BLK = 128
 HD = 128
-GROUP = 2
 
 masked_score = -1e30
 SCALE2 = math.log2(math.e) / math.sqrt(HD)
@@ -21,18 +20,26 @@
     slab, band = lax.axis_index("tm"), lax.axis_index("band")
     found = []
     if slab_count > 1:
-        found.append(({"tm": slab + 1}, slab < slab_count - 1, slab > 0, ("adj", 0)))
-        found.append(({"tm": slab - 1}, slab > 0, slab < slab_count - 1, ("adj", 1)))
+        found.append(({"tm": slab + 1}, slab < slab_count - 1, None, slab > 0, ("adj", 0)))
+        found.append(({"tm": slab - 1}, None, slab > 0, slab < slab_count - 1, ("adj", 1)))
     if band_count == 2:
-        found.append(({"band": 1 - band}, None, None, ("border", 1 - band)))
+        found.append(({"band": 1 - band}, band == 0, band == 1, None, ("border", 1 - band)))
     elif band_count > 2:
-        found.append(({"band": band + 1}, band < band_count - 1, band > 0, ("border", 1)))
-        found.append(({"band": band - 1}, band > 0, band < band_count - 1, ("border", 0)))
+        found.append(({"band": band + 1}, band < band_count - 1, None, band > 0, ("border", 1)))
+        found.append(({"band": band - 1}, None, band > 0, band < band_count - 1, ("border", 0)))
     return found
 
 
 def when(condition):
     return (lambda body: body()) if condition is None else pl.when(condition)
+
+
+def chunks_of(heads):
+    half = heads // 2
+    return (
+        [(0, half), (half, heads - half)],
+        [(0, half), (half, heads - half - 1), (heads - 1, 1)],
+    )
 
 
 def weigh(query, key):
@@ -45,51 +52,39 @@
 def kernel(
     slab_count, band_count, q_hbm, k_hbm, v_hbm, adj_hbm, border_hbm, out_ref,
     q_ref, k_ref, v_ref, adj_ref, border_ref, send_ref, recv_ref, acc_ref, weights_ref,
-    gain_ref, load_sem, send_sem, recv_sem,
+    gain_ref, load_sem, here_sem, send_sem, recv_sem,
 ):
     plan = routes(slab_count, band_count)
     rows, width = q_ref.shape
     heads = width // HD
-    groups = heads // GROUP
+
+    neighbours = []
+    for axis, count in (("tm", slab_count), ("band", band_count)):
+        if count > 1:
+            index = lax.axis_index(axis)
+            neighbours.append((axis, index, index > 0, index < count - 1))
 
     barrier = pltpu.get_barrier_semaphore()
-    for target, sends, _, _ in plan:
-        @when(sends)
+    for axis, index, _, has_upper in neighbours:
+        @pl.when(has_upper)
         def _():
-            pl.semaphore_signal(barrier, inc=1, device_id=target, device_id_type=MESH)
-
-    loads = []
-    for number, (source, target) in enumerate(
-        ((adj_hbm, adj_ref), (border_hbm, border_ref), (k_hbm, k_ref), (v_hbm, v_ref), (q_hbm, q_ref))
-    ):
-        copy = pltpu.make_async_copy(source, target, load_sem.at[number])
-        copy.start()
-        loads.append(copy)
-
-    for slot, (_, _, comes, _) in enumerate(plan):
-        if comes is not None:
-            @pl.when(jnp.logical_not(comes))
-            def _():
-                recv_ref[slot] = jnp.zeros(recv_ref.shape[1:], recv_ref.dtype)
-
-    loads[0].wait()
-    loads[1].wait()
-    starts = []
-    for _, _, _, (kind, row) in plan:
-        starts.append(adj_ref[row, 1] if kind == "adj" else border_ref[0, row])
-    for part, (load, whole) in enumerate(((loads[2], k_ref), (loads[3], v_ref))):
-        load.wait()
-        for slot in range(len(plan)):
-            for head in range(heads):
-                send_ref[slot, part, head] = whole[
-                    starts[slot], :, head * HD : (head + 1) * HD
-                ]
-
-    arrivals = sum(1 if comes is None else comes.astype(jnp.int32) for _, _, comes, _ in plan)
-    pl.semaphore_wait(barrier, arrivals)
+            pl.semaphore_signal(barrier, inc=1, device_id={axis: index + 1}, device_id_type=MESH)
+
+    picks = []
+    for number, (source, target) in enumerate(((adj_hbm, adj_ref), (border_hbm, border_ref))):
+        picks.append(pltpu.make_async_copy(source, target, load_sem.at[number]))
+    for pick in picks:
+        pick.start()
+    loads = [
+        pltpu.make_async_copy(source, target, load_sem.at[2 + number])
+        for number, (source, target) in enumerate(((k_hbm, k_ref), (v_hbm, v_ref), (q_hbm, q_ref)))
+    ]
+    loads[0].start()
+
+    chunks = chunks_of(heads)
 
     def transfer(slot, part, group):
-        at = (slot, part, pl.ds(group * GROUP, GROUP))
+        at = (slot, part, pl.ds(*chunks[part][group]))
         return pltpu.make_async_remote_copy(
             src_ref=send_ref.at[at],
             dst_ref=recv_ref.at[at],
@@ -99,14 +94,56 @@
             device_id_type=MESH,
         )
 
+    def send(part, downward):
+        for group in range(len(chunks[part])):
+            for slot, (_, up, down, _, _) in enumerate(plan):
+                sends = down if downward else up
+                if sends is not None:
+                    @pl.when(sends)
+                    def _():
+                        transfer(slot, part, group).start()
+
+    arrivals = sum(lower.astype(jnp.int32) for _, _, lower, _ in neighbours)
+
+    @pl.when(arrivals > 0)
+    def _():
+        pl.semaphore_wait(barrier, arrivals)
+
+    for number, (axis, index, has_lower, _) in enumerate(neighbours):
+        @pl.when(has_lower)
+        def _():
+            pl.semaphore_signal(
+                here_sem.at[number], inc=1, device_id={axis: index - 1}, device_id_type=MESH
+            )
+
+    for pick in picks:
+        pick.wait()
+    blocks = [
+        adj_ref[row, 1] if kind == "adj" else border_ref[0, row] for _, _, _, _, (kind, row) in plan
+    ]
+    for part, whole in enumerate((k_ref, v_ref)):
+        loads[part].wait()
+        if part == 0:
+            loads[1].start()
+            loads[2].start()
+        for slot in range(len(plan)):
+            for head in range(heads):
+                send_ref[slot, part, head] = whole[blocks[slot], :, head * HD : (head + 1) * HD]
+        send(part, True)
+    for number, (_, _, _, has_upper) in enumerate(neighbours):
+        @pl.when(has_upper)
+        def _():
+            pl.semaphore_wait(here_sem.at[number], 1)
     for part in range(2):
-        for group in range(groups):
-            for slot, (_, sends, _, _) in enumerate(plan):
-                @when(sends)
-                def _():
-                    transfer(slot, part, group).start()
-
-    loads[4].wait()
+        send(part, False)
+
+    for slot, (_, _, _, comes, _) in enumerate(plan):
+        if comes is not None:
+            @pl.when(jnp.logical_not(comes))
+            def _():
+                recv_ref[slot] = jnp.zeros(recv_ref.shape[1:], recv_ref.dtype)
+
+    loads[2].wait()
     own = []
     for head in range(heads):
         columns = slice(head * HD, (head + 1) * HD)
@@ -119,15 +156,15 @@
         )
         own.append((most, total))
 
-    for group in range(groups):
-        for slot, (_, _, comes, _) in enumerate(plan):
+    for group, (start, size) in enumerate(chunks[0]):
+        for slot, (_, _, _, comes, _) in enumerate(plan):
             @when(comes)
             def _():
                 transfer(slot, 0, group).wait_recv()
-        for head in range(group * GROUP, (group + 1) * GROUP):
+        for head in range(start, start + size):
             columns = slice(head * HD, (head + 1) * HD)
             pieces = [own[head]]
-            for slot, (_, _, comes, _) in enumerate(plan):
+            for slot, (_, _, _, comes, _) in enumerate(plan):
                 scores = weigh(q_ref[:, columns], recv_ref[slot, 0, head])
                 if comes is not None:
                     scores = scores + jnp.where(comes, 0.0, masked_score).astype(jnp.float32)
@@ -145,12 +182,12 @@
                     factors[slot + 1] / denominator, (rows, HD)
                 )
 
-    for group in range(groups):
-        for slot, (_, _, comes, _) in enumerate(plan):
+    for group, (start, size) in enumerate(chunks[1]):
+        for slot, (_, _, _, comes, _) in enumerate(plan):
             @when(comes)
             def _():
                 transfer(slot, 1, group).wait_recv()
-        for head in range(group * GROUP, (group + 1) * GROUP):
+        for head in range(start, start + size):
             result = acc_ref[head]
             for slot in range(len(plan)):
                 result = result + gain_ref[head, slot] * jnp.dot(
@@ -159,8 +196,10 @@
             out_ref[:, head * HD : (head + 1) * HD] = result.astype(out_ref.dtype)
 
     for part in range(2):
-        for group in range(groups):
-            for slot, (_, sends, _, _) in enumerate(plan):
+        for group in range(len(chunks[part])):
+            for slot, (_, up, down, _, _) in enumerate(plan):
+                sends = down if up is None else up if down is None else None
+
                 @when(sends)
                 def _():
                     transfer(slot, part, group).wait_send()
@@ -172,7 +211,7 @@
     slab_count, band_count = lax.axis_size("tm"), lax.axis_size("band")
     sources = (2 if slab_count > 1 else 0) + min(band_count - 1, 2)
     assert rows == 2 * BLK and adj_mask.shape[3] == 2 and border_blocks.shape[3] == 1
-    block_sems = pltpu.SemaphoreType.DMA((sources, 2, heads // GROUP))
+    block_sems = pltpu.SemaphoreType.DMA((sources, 2, max(map(len, chunks_of(heads)))))
     attended = pl.pallas_call(
         functools.partial(kernel, slab_count, band_count),
         out_shape=pltpu.VMEM((rows, width), jnp.bfloat16),
@@ -190,6 +229,7 @@
             pltpu.VMEM((heads, sources, rows, BLK), jnp.bfloat16),
             pltpu.VMEM((heads, sources, rows, HD), jnp.float32),
             pltpu.SemaphoreType.DMA((5,)),
+            pltpu.SemaphoreType.REGULAR((max(1, (slab_count > 1) + (band_count > 1)),)),
             block_sems,
             block_sems,
         ],

time: 15 us -> 14.8 us (0.987)
  Pallas kernels: 14.1 us -> 13.9 us
    pallas_call x1, Pallas kernels: 14.1 us -> 13.9 us  [per_device(): pl.pallas_call(functools.partial(kernel, slab_count, band_count), out_sha...]
where the time goes in v3:
time: 14.8 us; the launch traced here: 14.6 us
  Pallas kernels  13.9 us (94%)
  local copies, waits for them, and re-layouts  0.75 us (5%)
    pallas_call x1, Pallas kernels, per_device(): pl.pallas_call(functools.partial(kernel, slab_count, band_count), out_sha...  13.9 us
    unnamed x1, local copies, waits for them, and re-layouts  0.75 us

profile of v3, /device:TPU:0, one launch (start us, length us, event | category | flops | bytes accessed | tf_op | source)
XLA Modules:
  0.0 14.6 jit_solution(13862235753267197283)
XLA Ops:
  0.0 13.9 %radial_attention.1 = bf16[256,768]{1,0:T(8,128)(2,1)S(1)} custom-call(bf16[256,768]{1,0:T(8,128)(2,1)} %bitcast.7, bf16[2,128,768]{2,1,0:T(8,128)(2,1)} %bitcast.8, bf16[2,128,768]{2,1,0:T(8,128)(2,1)} %bitcast.9, s32[2,2]{1,0:T(2,128)} %bitcast.10, s32[1,2]{1,0:T(1,128)} %bitcast.11), custom_call_target="tpu_custom_call" | custom-call | tf_op jit(solution)/shard_map/radial_attention/pallas_call | solution.py:215
  13.9 0.7 %copy.7 = bf16[1,1,256,768]{3,2,1,0:T(8,128)(2,1)} copy(bf16[1,1,256,768]{3,2,1,0:T(8,128)(2,1)S(1)} %bitcast.6) | data formatting | bytes 786432

commit v4 on v3

--- a/solution.py
+++ b/solution.py
@@ -35,10 +35,9 @@
 
 
 def chunks_of(heads):
-    half = heads // 2
     return (
-        [(0, half), (half, heads - half)],
-        [(0, half), (half, heads - half - 1), (heads - 1, 1)],
+        [(0, heads)],
+        [(0, heads - 1), (heads - 1, 1)],
     )
 
 

time: 14.8 us -> 14.8 us (level)
  no operation moved by 1% of the time
where the time goes in v4:
time: 14.8 us; the launch traced here: 14.6 us
  Pallas kernels  13.8 us (93%)
  local copies, waits for them, and re-layouts  0.75 us (5%)
    pallas_call x1, Pallas kernels, per_device(): pl.pallas_call(functools.partial(kernel, slab_count, band_count), out_sha...  13.8 us
    unnamed x1, local copies, waits for them, and re-layouts  0.75 us

profile of v4, /device:TPU:0, one launch (start us, length us, event | category | flops | bytes accessed | tf_op | source)
XLA Modules:
  0.0 14.6 jit_solution(1902447765701113578)
XLA Ops:
  0.0 13.8 %radial_attention.1 = bf16[256,768]{1,0:T(8,128)(2,1)S(1)} custom-call(bf16[256,768]{1,0:T(8,128)(2,1)} %bitcast.7, bf16[2,128,768]{2,1,0:T(8,128)(2,1)} %bitcast.8, bf16[2,128,768]{2,1,0:T(8,128)(2,1)} %bitcast.9, s32[2,2]{1,0:T(2,128)} %bitcast.10, s32[1,2]{1,0:T(1,128)} %bitcast.11), custom_call_target="tpu_custom_call" | custom-call | tf_op jit(solution)/shard_map/radial_attention/pallas_call | solution.py:214
  13.8 0.7 %copy.7 = bf16[1,1,256,768]{3,2,1,0:T(8,128)(2,1)} copy(bf16[1,1,256,768]{3,2,1,0:T(8,128)(2,1)S(1)} %bitcast.6) | data formatting | bytes 786432
